TPU v7x, 32 devices: a whole 2x2x4 slice. The times are simulated.
32 devices in a mesh: tensor: 4 (over z), example: 8 (over y, x, core).
Axes of the slice: x: 2, y: 2, z: 4, core: 2. Of those that a mesh axis runs over, the one named last changes fastest.
Arguments:
- queries: bfloat16 [1, 4096, 4096], P(None, 'example', 'tensor'), may hold values from -0.0014648438 to 0.0014648438
- basis_out: bfloat16 [4096, 4096], P('example', 'tensor'), may hold values from -0.09375 to 0.09375
- basis_in: bfloat16 [4096, 4096], P('tensor', 'example'), may hold values from -0.09375 to 0.09375
- eigvals: float32 [4096, 4096], P('tensor', 'example'), may hold values from 0.25 to 4
- input_fac: bfloat16 [128, 8, 4096], P('example', None, 'tensor'), may hold values from -6 to 6
- grad_fac: bfloat16 [128, 8, 4096], P('example', None, 'tensor'), may hold values from -6 to 6
- cand_slot: int32 [128], replicated, may hold values from 0 to 127, as said below
- score_list: int32 [8, 16], replicated, may hold values from 0 to 127, as said below
- token_count: int32 [128], replicated, may hold values from 1 to 8
Outputs:
- scores: float32 [1, 128, 8], P(None, 'example')
Inputs may be any that keep to these rules, and one draw needn't show every extreme that they name: `cand_slot`: a permutation; slot s belongs to owner s // 16. `score_list`: every candidate appears exactly once; a scorer's list holds at most 4 candidates of any one owner, and some scorer takes exactly 4 from some owner.
All inputs are finite; a program needn't handle non-finite values.
Results may differ from a plain program's by a relative error of at most 0.019.
Values may be sent and summed in bfloat16 or wider, within the bound.
A program may use at most 128 MiB of HBM per device.

v0:
```python
import jax
import jax.numpy as jnp
from jax import lax
from jax.sharding import PartitionSpec as P


def body(
    queries, basis_out, basis_in, eigvals, input_fac, grad_fac, cand_slot, score_list, token_count
):
    ex_count = lax.axis_size("example")
    my_index = lax.axis_index("example")
    out_rows = lax.all_gather(basis_out, "tensor", axis=1, tiled=True)
    in_rows = lax.all_gather(basis_in, "example", axis=1, tiled=True)
    query_total = queries.shape[0]
    columns = out_rows
    rotated = lax.psum_scatter(
        jnp.einsum("ki,qkj->iqj", columns, queries, preferred_element_type=jnp.float32).astype(
            jnp.bfloat16
        ),
        "example",
        scatter_dimension=0,
        tiled=True,
    )
    columns = in_rows
    core_sum = lax.psum_scatter(
        jnp.einsum("kj,iqk->jqi", columns, rotated, preferred_element_type=jnp.float32).astype(
            jnp.bfloat16
        ),
        "tensor",
        scatter_dimension=0,
        tiled=True,
    ).astype(jnp.float32)
    scaled = (core_sum / eigvals[:, None, :]).astype(jnp.bfloat16)
    columns = out_rows
    turned = jnp.einsum(
        "jqk,ik->jqi",
        lax.all_gather(scaled, "example", axis=2, tiled=True),
        columns,
        preferred_element_type=jnp.float32,
    ).astype(jnp.bfloat16)
    columns = in_rows
    precond = jnp.einsum(
        "jk,kqi->jqi",
        columns,
        lax.all_gather(turned, "tensor", axis=0, tiled=True),
        preferred_element_type=jnp.float32,
    ).astype(jnp.bfloat16)
    cand_total = cand_slot.shape[0]
    cand_dev = input_fac.shape[0]
    token_len = input_fac.shape[1]
    shard_width = input_fac.shape[2]
    list_len = score_list.shape[1]
    cand_ids = jnp.arange(cand_total, dtype=jnp.int32)
    matches = (score_list[:, :, None] == cand_ids[None, None, :]).astype(jnp.int32)
    entry_slot = jnp.sum(matches * cand_slot[None, None, :], axis=2)
    entry_count = jnp.sum(matches * token_count[None, None, :], axis=2)
    entry_owner = entry_slot // cand_dev
    entry_local = entry_slot % cand_dev
    earlier = jnp.arange(list_len)[:, None] > jnp.arange(list_len)[None, :]
    same_owner = entry_owner[:, :, None] == entry_owner[:, None, :]
    entry_rank = jnp.sum((same_owner & earlier[None]).astype(jnp.int32), axis=2)
    capacity = 2 * cand_dev // ex_count
    place_ids = jnp.arange(capacity, dtype=jnp.int32)
    local_ids = jnp.arange(cand_dev, dtype=jnp.int32)
    owned_here = entry_owner == my_index
    send_table = jnp.sum(
        (
            owned_here[:, :, None, None]
            & (entry_rank[:, :, None, None] == place_ids[None, None, :, None])
            & (entry_local[:, :, None, None] == local_ids[None, None, None, :])
        ).astype(jnp.float32),
        axis=1,
    )
    my_owner = lax.dynamic_index_in_dim(entry_owner, my_index, 0, keepdims=False)
    my_rank = lax.dynamic_index_in_dim(entry_rank, my_index, 0, keepdims=False)
    my_count = lax.dynamic_index_in_dim(entry_count, my_index, 0, keepdims=False)
    source_ids = jnp.arange(ex_count, dtype=jnp.int32)
    take_table = (
        (
            (my_owner[:, None, None] == source_ids[None, :, None])
            & (my_rank[:, None, None] == place_ids[None, None, :])
        )
        .astype(jnp.float32)
        .reshape(list_len, ex_count * capacity)
    )
    select_send = send_table.astype(jnp.bfloat16)
    select_take = take_table.astype(jnp.bfloat16)

    def route_rows(owned_rows):
        return jnp.einsum(
            "ers,sx->erx", select_send, owned_rows, preferred_element_type=jnp.float32
        ).astype(jnp.bfloat16)

    def collect_rows(received):
        flat_received = received.reshape(ex_count * capacity, received.shape[2])
        return jnp.dot(select_take, flat_received, preferred_element_type=jnp.float32).astype(
            jnp.bfloat16
        )

    flat_acts = input_fac.reshape(cand_dev, token_len * shard_width)
    flat_grads = grad_fac.reshape(cand_dev, token_len * shard_width)
    sent_acts, sent_grads = (
        lax.all_to_all(route_rows(flat_acts), "example", split_axis=0, concat_axis=0, tiled=True),
        lax.all_to_all(route_rows(flat_grads), "example", split_axis=0, concat_axis=0, tiled=True),
    )
    got_acts = collect_rows(sent_acts).reshape(list_len * token_len, shard_width)
    got_grads = collect_rows(sent_grads).reshape(list_len * token_len, shard_width)
    whole_grads = lax.all_gather(got_grads, "tensor", axis=1, tiled=True)
    columns = whole_grads
    weighted = jnp.einsum(
        "tn,jqn->qtj",
        columns,
        lax.all_gather(precond, "example", axis=2, tiled=True),
        preferred_element_type=jnp.float32,
    )
    partial_scores = jnp.sum(got_acts.astype(jnp.float32)[None] * weighted, axis=2)
    summed = lax.psum(partial_scores, "tensor").reshape(query_total, list_len, token_len)
    live_mask = jnp.arange(token_len, dtype=jnp.int32)[None, :] < my_count[:, None]
    return jnp.where(live_mask[None], summed, jnp.float32(0.0))


def solution(mesh):
    in_specs = (
        P(None, "example", "tensor"),
        P("example", "tensor"),
        P("tensor", "example"),
        P("tensor", "example"),
        P("example", None, "tensor"),
        P("example", None, "tensor"),
        P(),
        P(),
        P(),
    )
    out_specs = P(None, "example", None)
    return jax.shard_map(body, mesh=mesh, in_specs=in_specs, out_specs=out_specs, check_vma=False)
```

profile of v0, /device:TPU:0, one launch (start us, length us, event | category | flops | bytes accessed | tf_op | source)
XLA Modules:
  0.0 568.8 jit_solution(2000959011714621672)
XLA Ops:
  6.5 0.0 copy-start
  6.5 0.0 all-gather.9.cloned.1.call-start
  6.5 0.7 all-gather.9.cloned.1.call-update
  7.3 0.0 all-gather.11.cloned.1.call-start
  7.3 0.7 all-gather.11.cloned.1.call-update
  8.0 0.0 reduce-scatter.3.cloned.1.call-start
  8.1 84.4 %all-gather.9.cloned.1.call-done = bf16[512,4096]{1,0:T(8,128)(2,1)} async-done(((bf16[512,1024]{1,0:T(8,128)(2,1)}), bf16[512,4096]{1,0:T(8,128)(2,1)}) %all-gather.9.cloned.1.call-update) | async-done | bytes 4194320 | tf_op jit(solution)/shard_map/all_gather | solution.py:12
  92.4 0.0 copy-done
  92.4 9.0 %convert_bitcast_fusion = bf16[4096,1,1024]{2,0,1:T(8,128)(2,1)} fusion(bf16[512,4096]{1,0:T(8,128)(2,1)} %all-gather.9.cloned.1.call-done, bf16[1,512,1024]{2,1,0:T(8,128)(2,1)S(1)} %copy-done), kind=kOutput, calls=%fused_computation.9 | convolution fusion | flops 4299161600 | bytes 13631488 | tf_op jit(solution)/shard_map/ki,qkj->iqj/dot_general | solution.py:17
  101.4 0.0 reduce-scatter.3.cloned.1.call-update
  101.4 0.0 reduce-scatter.5.cloned.1.call-start
  101.5 47.3 %all-gather.11.cloned.1.call-done = bf16[1024,4096]{1,0:T(8,128)(2,1)} async-done(((bf16[1024,512]{1,0:T(8,128)(2,1)}), bf16[1024,4096]{1,0:T(8,128)(2,1)}) %all-gather.11.cloned.1.call-update) | async-done | bytes 8388624 | tf_op jit(solution)/shard_map/all_gather | solution.py:13
  148.8 74.8 %reduce-scatter.3.cloned.1.call-done = bf16[512,1,1024]{2,0,1:T(8,128)(2,1)} async-done(((bf16[4096,1,1024]{2,0,1:T(8,128)(2,1)}), bf16[512,1,1024]{2,0,1:T(8,128)(2,1)}) %reduce-scatter.3.cloned.1.call-update) | async-done | bytes 1048592 | tf_op jit(solution)/shard_map/reduce_scatter | solution.py:16
  223.6 10.2 %fusion.5 = bf16[4096,1,512]{0,2,1:T(8,128)(2,1)} fusion(bf16[1024,4096]{1,0:T(8,128)(2,1)} %all-gather.11.cloned.1.call-done, bf16[512,1,1024]{2,0,1:T(8,128)(2,1)} %reduce-scatter.3.cloned.1.call-done), kind=kOutput, calls=%fused_computation.11 | convolution fusion | flops 4297064448 | bytes 13631488 | tf_op jit(solution)/shard_map/kj,iqk->jqi/dot_general | solution.py:26
  233.8 0.0 reduce-scatter.5.cloned.1.call-update
  233.8 0.0 all-gather.13.cloned.1.call-start
  233.9 1.9 copy.26
  235.8 74.9 %reduce-scatter.5.cloned.1.call-done = bf16[1024,1,512]{0,2,1:T(8,128)(2,1)} async-done(((bf16[4096,1,512]{0,2,1:T(8,128)(2,1)}), bf16[1024,1,512]{0,2,1:T(8,128)(2,1)}) %reduce-scatter.5.cloned.1.call-update) | async-done | bytes 1048592 | tf_op jit(solution)/shard_map/reduce_scatter | solution.py:25
  310.7 2.6 fusion.6
  313.3 0.0 all-gather.13.cloned.1.call-update
  313.4 0.0 copy-start.1
  313.4 0.0 copy-start.3
  313.4 0.0 copy-start.4
  313.4 0.0 copy-start.5
  313.4 0.2 all-gather.17.cloned.1.call-start
  313.6 54.8 %all-gather.13.cloned.1.call-done = bf16[1024,1,4096]{0,2,1:T(8,128)(2,1)} async-done(((bf16[1024,1,512]{0,2,1:T(8,128)(2,1)}), bf16[1024,1,4096]{0,2,1:T(8,128)(2,1)}) %all-gather.13.cloned.1.call-update) | async-done | bytes 8388624 | tf_op jit(solution)/shard_map/all_gather | solution.py:37
  368.4 10.1 %fusion.7 = bf16[1024,512]{1,0:T(8,128)(2,1)} fusion(bf16[512,4096]{1,0:T(8,128)(2,1)} %all-gather.9.cloned.1.call-done, bf16[1024,1,4096]{0,2,1:T(8,128)(2,1)} %all-gather.13.cloned.1.call-done), kind=kOutput, calls=%fused_computation.14 | convolution fusion | flops 4295491584 | bytes 13631488 | tf_op jit(solution)/shard_map/jqk,ik->jqi/dot_general | solution.py:35
  378.5 0.0 all-gather.17.cloned.1.call-update
  378.5 0.0 copy-done.1
  378.5 0.1 reshape.275
  378.7 0.0 copy-done.3
  378.7 0.0 copy-done.4
  378.7 0.4 select_reduce_fusion.1
  379.1 0.3 convert_reduce_fusion.1
  379.5 0.1 iota_compare_fusion
  379.5 0.2 convert_reduce_fusion
  379.7 0.3 convolution_convert_fusion
  380.0 1.2 copy.28
  381.2 3.5 all-to-all-start.1
  384.7 0.0 all-gather.15.cloned.1.call-start
  384.8 9.6 %all-to-all-done.1 = bf16[8,4,8192]{2,1,0:T(4,128)(2,1)S(1)} async-done(((bf16[8,4,8192]{2,1,0:T(4,128)(2,1)}), bf16[8,4,8192]{2,1,0:T(4,128)(2,1)S(1)}, u32[]{:S(2)}, u32[]{:S(2)}) %all-to-all-start.1) | async-done | bytes 524320 | tf_op jit(solution)/shard_map/all_to_all | solution.py:104
  394.4 0.4 fusion.2
  394.8 0.9 reshape.265
  395.6 0.0 all-gather.15.cloned.1.call-update
  395.7 0.0 copy-start.2
  395.7 0.3 all-gather.19.cloned.1.call-start
  396.0 63.5 %all-gather.17.cloned.1.call-done = bf16[4096,512]{1,0:T(8,128)(2,1)} async-done(((bf16[1024,512]{1,0:T(8,128)(2,1)}), bf16[4096,512]{1,0:T(8,128)(2,1)}) %all-gather.17.cloned.1.call-update) | async-done | bytes 4194320 | tf_op jit(solution)/shard_map/all_gather | solution.py:45
  459.4 10.2 %fusion.10 = bf16[1024,512]{0,1:T(8,128)(2,1)} fusion(bf16[4096,512]{1,0:T(8,128)(2,1)} %all-gather.17.cloned.1.call-done, bf16[1024,4096]{1,0:T(8,128)(2,1)} %all-gather.11.cloned.1.call-done), kind=kOutput, calls=%fused_computation.16 | convolution fusion | flops 4295491584 | bytes 13631488 | tf_op jit(solution)/shard_map/jk,kqi->jqi/dot_general | solution.py:42
  469.6 0.0 all-gather.19.cloned.1.call-update
  469.6 0.1 reshape.273
  469.8 0.3 convolution_convert_fusion.1
  470.1 1.2 copy.24
  471.3 3.7 all-to-all-start
  475.0 9.7 %all-to-all-done = bf16[8,4,8192]{2,1,0:T(4,128)(2,1)S(1)} async-done(((bf16[8,4,8192]{2,1,0:T(4,128)(2,1)}), bf16[8,4,8192]{2,1,0:T(4,128)(2,1)S(1)}, u32[]{:S(2)}, u32[]{:S(2)}) %all-to-all-start) | async-done | bytes 524320 | tf_op jit(solution)/shard_map/all_to_all | solution.py:103
  484.7 0.4 fusion.1
  485.1 0.1 reshape.268
  485.3 0.2 copy.30
  485.4 2.0 all-gather.15.cloned.1.call-done
  487.5 55.8 %all-gather.19.cloned.1.call-done = bf16[1024,4096]{0,1:T(8,128)(2,1)} async-done(((bf16[1024,512]{0,1:T(8,128)(2,1)}), bf16[1024,4096]{0,1:T(8,128)(2,1)}) %all-gather.19.cloned.1.call-update) | async-done | bytes 8388624 | tf_op jit(solution)/shard_map/all_gather | solution.py:113
  543.3 6.0 %fusion.12 = f32[128]{0:T(128)S(1)} fusion(f32[1,128,1024]{1,2,0:T(8,128)S(1)} %copy.30, bf16[1024,4096]{0,1:T(8,128)(2,1)} %all-gather.19.cloned.1.call-done, bf16[128,4096]{1,0:T(8,128)(2,1)} %all-gather.15.cloned.1.call-done), kind=kOutput, calls=%fused_computation.19 | convolution fusion | flops 1074003840 | bytes 9961984 | tf_op jit(solution)/shard_map/tn,jqn->qtj/dot_general | solution.py:110
  549.3 0.1 reshape.266
  549.4 11.8 %psum.7 = f32[1,16,8]{2,1,0:T(8,128)S(1)} all-reduce(f32[1,16,8]{2,1,0:T(8,128)S(1)} %reshape.266), channel_id=1, replica_groups=mesh['tensor'=4,'example'=8] {'tensor'}, use_global_device_ids=true, to_apply=%region_7.8 | all-reduce | flops 128 | bytes 1024 | tf_op jit(solution)/shard_map/psum | solution.py:117
  561.2 0.1 fusion.18
  561.3 0.7 copy.31
  (10 shorter events, 0.1 us)
Async XLA Ops:
  6.5 85.9 %copy-start = (bf16[1,512,1024]{2,1,0:T(8,128)(2,1)S(1)}, bf16[1,512,1024]{2,1,0:T(8,128)(2,1)}, u32[]{:S(2)}) copy-start(bf16[1,512,1024]{2,1,0:T(8,128)(2,1)} %param.9) | copy-start | bytes 3145732
  6.5 85.9 %all-gather.9.cloned.1.call-start = ((), (), s32[]{:S(2)}) async-start(), calls=%async_computation.4 | async-start | bytes 5242880 | tf_op jit(solution)/shard_map/all_gather | solution.py:12
  7.3 141.6 %all-gather.11.cloned.1.call-start = ((), (), s32[]{:S(2)}) async-start(), calls=%async_computation.6 | async-start | bytes 9437184 | tf_op jit(solution)/shard_map/all_gather | solution.py:13
  8.0 215.6 %reduce-scatter.3.cloned.1.call-start = ((), (), s32[]{:S(2)}) async-start(), calls=%async_computation.5 | async-start | bytes 9437184 | tf_op jit(solution)/shard_map/reduce_scatter | solution.py:16
  101.4 209.3 %reduce-scatter.5.cloned.1.call-start = ((), (), s32[]{:S(2)}) async-start(), calls=%async_computation.7 | async-start | bytes 5242880 | tf_op jit(solution)/shard_map/reduce_scatter | solution.py:25
  233.8 134.6 %all-gather.13.cloned.1.call-start = ((), (), s32[]{:S(2)}) async-start(), calls=%async_computation.8 | async-start | bytes 9437184 | tf_op jit(solution)/shard_map/all_gather | solution.py:37
  313.4 65.1 %copy-start.1 = (bf16[16,8,1024]{2,1,0:T(8,128)(2,1)S(1)}, bf16[16,8,1024]{2,1,0:T(8,128)(2,1)}, u32[]{:S(2)}) copy-start(bf16[16,8,1024]{2,1,0:T(8,128)(2,1)} %param.14) | copy-start | bytes 786436
  313.4 65.3 %copy-start.3 = (s32[8,16]{1,0:T(8,128)S(1)}, s32[8,16]{1,0:T(8,128)}, u32[]{:S(2)}) copy-start(s32[8,16]{1,0:T(8,128)} %param.16) | copy-start | bytes 1540
  313.4 65.3 %copy-start.4 = (s32[128]{0:T(128)S(1)}, s32[128]{0:T(128)}, u32[]{:S(2)}) copy-start(s32[128]{0:T(128)} %param.17) | copy-start | bytes 1540
  313.4 65.3 %copy-start.5 = (s32[128]{0:T(128)S(1)}, s32[128]{0:T(128)}, u32[]{:S(2)}) copy-start(s32[128]{0:T(128)} %param.15) | copy-start | bytes 1540
  313.4 146.0 %all-gather.17.cloned.1.call-start = ((), (), s32[]{:S(2)}) async-start(), calls=%async_computation.10 | async-start | bytes 5242880 | tf_op jit(solution)/shard_map/all_gather | solution.py:45
  381.2 13.2 %all-to-all-start.1 = ((bf16[8,4,8192]{2,1,0:T(4,128)(2,1)}), bf16[8,4,8192]{2,1,0:T(4,128)(2,1)S(1)}, u32[]{:S(2)}, u32[]{:S(2)}) async-start(bf16[8,4,8192]{2,1,0:T(4,128)(2,1)} %copy.28), calls=%async_computation.3 | async-start | bytes 1048576 | tf_op jit(solution)/shard_map/all_to_all | solution.py:104
  384.7 102.8 %all-gather.15.cloned.1.call-start = ((), (), s32[]{:S(2)}) async-start(), calls=%async_computation.9 | async-start | bytes 1310720 | tf_op jit(solution)/shard_map/all_gather | solution.py:108
  395.7 74.0 %copy-start.2 = (bf16[16,8,1024]{2,1,0:T(8,128)(2,1)S(1)}, bf16[16,8,1024]{2,1,0:T(8,128)(2,1)}, u32[]{:S(2)}) copy-start(bf16[16,8,1024]{2,1,0:T(8,128)(2,1)} %param.13) | copy-start | bytes 786436
  395.7 147.6 %all-gather.19.cloned.1.call-start = ((), (), s32[]{:S(2)}) async-start(), calls=%async_computation.11 | async-start | bytes 9437184 | tf_op jit(solution)/shard_map/all_gather | solution.py:113
  471.3 13.4 %all-to-all-start = ((bf16[8,4,8192]{2,1,0:T(4,128)(2,1)}), bf16[8,4,8192]{2,1,0:T(4,128)(2,1)S(1)}, u32[]{:S(2)}, u32[]{:S(2)}) async-start(bf16[8,4,8192]{2,1,0:T(4,128)(2,1)} %copy.24), calls=%async_computation | async-start | bytes 1048576 | tf_op jit(solution)/shard_map/all_to_all | solution.py:103
Sparse Core Ops, SparseCore 0:
  8.9 83.4 all-gather.8
  94.3 54.4 all-gather.10
  152.3 71.2 reduce-scatter.2
  233.9 76.7 reduce-scatter.4
  313.5 54.8 all-gather.12
  378.6 80.7 all-gather.16
  461.0 26.4 all-gather.14
  489.4 53.8 all-gather.18
where the time goes:
time: 569 us
  waiting for transfers between devices  478 us (84%)
  matrix products  46.8 us (8%)
  between operations  13.7 us (2%)
  blocking collectives  11.8 us (2%)
  starting transfers between devices  7.87 us (1%)
  local copies, waits for them, and re-layouts  6.58 us (1%)
    all_gather x1, waiting for transfers between devices, body(): out_rows = lax.all_gather(basis_out, 'tensor', axis=1, tiled=True)  84.4 us
    reduce_scatter x1, waiting for transfers between devices, body(): lax.psum_scatter(jnp.einsum('kj,iqk->jqi', columns, rotated, preferred_el...  74.9 us
    reduce_scatter x1, waiting for transfers between devices, body(): lax.psum_scatter(jnp.einsum('ki,qkj->iqj', columns, queries, preferred_el...  74.8 us
    all_gather x1, waiting for transfers between devices, body(): lax.all_gather(turned, 'tensor', axis=0, tiled=True)  63.5 us
    all_gather x1, waiting for transfers between devices, body(): lax.all_gather(precond, 'example', axis=2, tiled=True)  55.8 us
    all_gather x1, waiting for transfers between devices, body(): lax.all_gather(scaled, 'example', axis=2, tiled=True)  54.8 us
    all_gather x1, waiting for transfers between devices, body(): in_rows = lax.all_gather(basis_in, 'example', axis=1, tiled=True)  47.3 us
    psum x1, blocking collectives, body(): lax.psum(partial_scores, 'tensor').reshape(query_total, list_len, token_len)  11.8 us
  transfers between devices with their start and end apart: 10, of which 10 were waited for; matrix products, arithmetic and copies ran while one was open for 5% of the time, Pallas kernels for 0%

commit v1 on v0

--- a/solution.py
+++ b/solution.py
@@ -2,6 +2,18 @@
 import jax.numpy as jnp
 from jax import lax
 from jax.sharding import PartitionSpec as P
+
+
+def doubled_up(shard, axis, dim):
+    ways, here, step = (lax.axis_size(axis), lax.axis_index(axis), shard.shape[dim])
+    line, have = (shard, 1)
+    while have < ways:
+        line = jnp.concatenate(
+            [line, lax.ppermute(line, axis, [(d, (d - have) % ways) for d in range(ways)])],
+            axis=dim,
+        )
+        have = 2 * have
+    return jnp.roll(line, here * step, axis=dim)
 
 
 def body(
@@ -33,10 +45,7 @@
     scaled = (core_sum / eigvals[:, None, :]).astype(jnp.bfloat16)
     columns = out_rows
     turned = jnp.einsum(
-        "jqk,ik->jqi",
-        lax.all_gather(scaled, "example", axis=2, tiled=True),
-        columns,
-        preferred_element_type=jnp.float32,
+        "jqk,ik->jqi", doubled_up(scaled, "example", 2), columns, preferred_element_type=jnp.float32
     ).astype(jnp.bfloat16)
     columns = in_rows
     precond = jnp.einsum(

time: 569 us -> 682 us (1.20)
  waiting for transfers between devices: 478 us -> 571 us
  local copies, waits for them, and re-layouts: 6.58 us -> 23.2 us
    ppermute x0 -> x3, waiting for transfers between devices: none -> 148 us  [doubled_up(): lax.ppermute(line, axis, [(d, (d - have) % ways) for d in range(ways)])]
    all_gather x1 -> x0, waiting for transfers between devices: 54.8 us -> none  [body(): lax.all_gather(scaled, 'example', axis=2, tiled=True)]
    unnamed x13 -> x27, local copies, waits for them, and re-layouts: 1.96 us -> 14.1 us
  transfers between devices with their start and end apart: 10 -> 12, of which waited for: 10 -> 12; matrix products, arithmetic and copies ran while one was open for 5% -> 5% of each run, Pallas kernels for 0% -> 0%
where the time goes in v1:
time: 682 us
  waiting for transfers between devices  571 us (84%)
  matrix products  45.1 us (7%)
  local copies, waits for them, and re-layouts  23.2 us (3%)
  between operations  13.7 us (2%)
  blocking collectives  11.8 us (2%)
  starting transfers between devices  10.8 us (2%)
    ppermute x3, waiting for transfers between devices, doubled_up(): lax.ppermute(line, axis, [(d, (d - have) % ways) for d in range(ways)])  148 us
    all_gather x1, waiting for transfers between devices, body(): out_rows = lax.all_gather(basis_out, 'tensor', axis=1, tiled=True)  84.4 us
    reduce_scatter x1, waiting for transfers between devices, body(): lax.psum_scatter(jnp.einsum('kj,iqk->jqi', columns, rotated, preferred_el...  74.9 us
    reduce_scatter x1, waiting for transfers between devices, body(): lax.psum_scatter(jnp.einsum('ki,qkj->iqj', columns, queries, preferred_el...  74.8 us
    all_gather x1, waiting for transfers between devices, body(): lax.all_gather(turned, 'tensor', axis=0, tiled=True)  62.7 us
    all_gather x1, waiting for transfers between devices, body(): lax.all_gather(precond, 'example', axis=2, tiled=True)  55.8 us
    all_gather x1, waiting for transfers between devices, body(): in_rows = lax.all_gather(basis_in, 'example', axis=1, tiled=True)  47.3 us
    unnamed x27, local copies, waits for them, and re-layouts  14.1 us
  transfers between devices with their start and end apart: 12, of which 12 were waited for; matrix products, arithmetic and copies ran while one was open for 5% of the time, Pallas kernels for 0%

profile of v1, /device:TPU:0, one launch (start us, length us, event | category | flops | bytes accessed | tf_op | source)
XLA Modules:
  0.0 681.6 jit_solution(3922233767656994828)
XLA Ops:
  6.5 0.7 all-gather.8.cloned.1.call-update
  7.3 0.0 all-gather.10.cloned.1.call-start
  7.3 0.7 all-gather.10.cloned.1.call-update
  8.0 0.0 reduce-scatter.3.cloned.1.call-start
  8.1 84.4 %all-gather.8.cloned.1.call-done = bf16[512,4096]{1,0:T(8,128)(2,1)} async-done(((bf16[512,1024]{1,0:T(8,128)(2,1)}), bf16[512,4096]{1,0:T(8,128)(2,1)}) %all-gather.8.cloned.1.call-update) | async-done | bytes 4194320 | tf_op jit(solution)/shard_map/all_gather | solution.py:24
  92.4 9.0 %convert_bitcast_fusion = bf16[4096,1,1024]{2,0,1:T(8,128)(2,1)} fusion(bf16[512,4096]{1,0:T(8,128)(2,1)} %all-gather.8.cloned.1.call-done, bf16[1,512,1024]{2,1,0:T(8,128)(2,1)S(1)} %copy-done), kind=kOutput, calls=%fused_computation.10 | convolution fusion | flops 4299161600 | bytes 13631488 | tf_op jit(solution)/shard_map/ki,qkj->iqj/dot_general | solution.py:29
  101.5 0.0 reduce-scatter.3.cloned.1.call-update
  101.5 0.0 reduce-scatter.5.cloned.1.call-start
  101.5 47.3 %all-gather.10.cloned.1.call-done = bf16[1024,4096]{1,0:T(8,128)(2,1)} async-done(((bf16[1024,512]{1,0:T(8,128)(2,1)}), bf16[1024,4096]{1,0:T(8,128)(2,1)}) %all-gather.10.cloned.1.call-update) | async-done | bytes 8388624 | tf_op jit(solution)/shard_map/all_gather | solution.py:25
  148.8 74.8 %reduce-scatter.3.cloned.1.call-done = bf16[512,1,1024]{2,0,1:T(8,128)(2,1)} async-done(((bf16[4096,1,1024]{2,0,1:T(8,128)(2,1)}), bf16[512,1,1024]{2,0,1:T(8,128)(2,1)}) %reduce-scatter.3.cloned.1.call-update) | async-done | bytes 1048592 | tf_op jit(solution)/shard_map/reduce_scatter | solution.py:28
  223.6 10.2 %fusion.6 = bf16[4096,1,512]{0,2,1:T(8,128)(2,1)} fusion(bf16[1024,4096]{1,0:T(8,128)(2,1)} %all-gather.10.cloned.1.call-done, bf16[512,1,1024]{2,0,1:T(8,128)(2,1)} %reduce-scatter.3.cloned.1.call-done), kind=kOutput, calls=%fused_computation.12 | convolution fusion | flops 4297064448 | bytes 13631488 | tf_op jit(solution)/shard_map/kj,iqk->jqi/dot_general | solution.py:38
  233.8 0.0 reduce-scatter.5.cloned.1.call-update
  233.8 0.0 all-gather.14.cloned.1.call-start
  233.9 1.9 copy.26
  235.8 74.9 %reduce-scatter.5.cloned.1.call-done = bf16[1024,1,512]{0,2,1:T(8,128)(2,1)} async-done(((bf16[4096,1,512]{0,2,1:T(8,128)(2,1)}), bf16[1024,1,512]{0,2,1:T(8,128)(2,1)}) %reduce-scatter.5.cloned.1.call-update) | async-done | bytes 1048592 | tf_op jit(solution)/shard_map/reduce_scatter | solution.py:37
  310.7 2.7 constant_dynamic-update-slice_fusion.7
  313.5 1.8 collective-permute-start
  315.3 12.3 %collective-permute-done = bf16[1024,1,512]{0,2,1:T(8,128)(2,1)S(1)} collective-permute-done((bf16[1024,1,512]{0,2,1:T(8,128)(2,1)S(1)}, bf16[1024,1,512]{0,2,1:T(8,128)(2,1)S(1)}, u32[]{:S(2)}, u32[]{:S(2)}) %collective-permute-start) | collective-permute-done | bytes 1048608 | tf_op jit(solution)/shard_map/ppermute | solution.py:12
  327.6 0.3 pad_maximum_fusion.1
  327.9 0.8 collective-permute-start.1
  328.7 47.5 %collective-permute-done.1 = bf16[1024,1,1024]{0,2,1:T(8,128)(2,1)S(1)} collective-permute-done((bf16[1024,1,1024]{0,2,1:T(8,128)(2,1)S(1)}, bf16[1024,1,1024]{0,2,1:T(8,128)(2,1)S(1)}, u32[]{:S(2)}, u32[]{:S(2)}) %collective-permute-start.1) | collective-permute-done | bytes 2097184 | tf_op jit(solution)/shard_map/ppermute | solution.py:12
  376.2 2.3 pad_maximum_fusion
  378.5 0.5 collective-permute-start.2
  379.1 2.4 constant_dynamic-update-slice_fusion.6
  381.5 1.5 constant_dynamic-update-slice_fusion.5
  382.9 88.2 %collective-permute-done.2 = bf16[1024,1,2048]{0,2,1:T(8,128)(2,1)} collective-permute-done((bf16[1024,1,2048]{0,2,1:T(8,128)(2,1)}, bf16[1024,1,2048]{0,2,1:T(8,128)(2,1)}, u32[]{:S(2)}, u32[]{:S(2)}) %collective-permute-start.2) | collective-permute-done | bytes 4194336 | tf_op jit(solution)/shard_map/ppermute | solution.py:12
  471.1 4.6 constant_dynamic-update-slice_fusion.4
  475.7 1.1 constant_dynamic-update-slice_fusion.3
  476.8 1.1 constant_dynamic-update-slice_fusion.2
  477.9 1.5 constant_dynamic-update-slice_fusion.1
  479.4 4.6 constant_dynamic-update-slice_fusion
  484.0 8.3 %fusion.8 = bf16[1024,512]{1,0:T(8,128)(2,1)} fusion(bf16[512,4096]{1,0:T(8,128)(2,1)S(1)} %copy-done.9, bf16[1024,1,8192]{0,2,1:T(8,128)(2,1)} %constant_dynamic-update-slice_fusion, s32[]{:T(128)S(6)} %select_n.62), kind=kOutput, calls=%fused_computation.17 | convolution fusion | flops 4295491584 | bytes 13631492 | tf_op jit(solution)/shard_map/jqk,ik->jqi/dot_general | solution.py:47
  492.3 0.0 all-gather.14.cloned.1.call-update
  492.3 0.1 reshape.275
  492.5 0.4 select_reduce_fusion.1
  492.9 0.3 convert_reduce_fusion.1
  493.3 0.1 iota_compare_fusion
  493.4 0.2 convert_reduce_fusion
  493.5 0.3 convolution_convert_fusion
  493.8 1.2 copy.28
  495.0 3.5 all-to-all-start.1
  498.5 0.0 all-gather.12.cloned.1.call-start
  498.6 9.6 %all-to-all-done.1 = bf16[8,4,8192]{2,1,0:T(4,128)(2,1)S(1)} async-done(((bf16[8,4,8192]{2,1,0:T(4,128)(2,1)}), bf16[8,4,8192]{2,1,0:T(4,128)(2,1)S(1)}, u32[]{:S(2)}, u32[]{:S(2)}) %all-to-all-start.1) | async-done | bytes 524320 | tf_op jit(solution)/shard_map/all_to_all | solution.py:113
  508.2 0.4 fusion.2
  508.6 0.8 reshape.265
  509.4 0.0 all-gather.12.cloned.1.call-update
  509.4 0.3 all-gather.16.cloned.1.call-start
  509.7 62.7 %all-gather.14.cloned.1.call-done = bf16[4096,512]{1,0:T(8,128)(2,1)} async-done(((bf16[1024,512]{1,0:T(8,128)(2,1)}), bf16[4096,512]{1,0:T(8,128)(2,1)}) %all-gather.14.cloned.1.call-update) | async-done | bytes 4194320 | tf_op jit(solution)/shard_map/all_gather | solution.py:54
  572.4 10.2 %fusion.11 = bf16[1024,512]{0,1:T(8,128)(2,1)} fusion(bf16[4096,512]{1,0:T(8,128)(2,1)} %all-gather.14.cloned.1.call-done, bf16[1024,4096]{1,0:T(8,128)(2,1)} %all-gather.10.cloned.1.call-done), kind=kOutput, calls=%fused_computation.19 | convolution fusion | flops 4295491584 | bytes 13631488 | tf_op jit(solution)/shard_map/jk,kqi->jqi/dot_general | solution.py:51
  582.6 0.1 reshape.273
  582.8 0.3 convolution_convert_fusion.1
  583.0 1.2 copy.24
  584.2 3.7 all-to-all-start
  587.9 9.7 %all-to-all-done = bf16[8,4,8192]{2,1,0:T(4,128)(2,1)S(1)} async-done(((bf16[8,4,8192]{2,1,0:T(4,128)(2,1)}), bf16[8,4,8192]{2,1,0:T(4,128)(2,1)S(1)}, u32[]{:S(2)}, u32[]{:S(2)}) %all-to-all-start) | async-done | bytes 524320 | tf_op jit(solution)/shard_map/all_to_all | solution.py:112
  597.7 0.4 fusion.1
  598.1 0.1 reshape.268
  598.2 0.2 copy.30
  598.4 1.9 all-gather.12.cloned.1.call-done
  600.3 55.8 %all-gather.16.cloned.1.call-done = bf16[1024,4096]{0,1:T(8,128)(2,1)} async-done(((bf16[1024,512]{0,1:T(8,128)(2,1)}), bf16[1024,4096]{0,1:T(8,128)(2,1)}) %all-gather.16.cloned.1.call-update) | async-done | bytes 8388624 | tf_op jit(solution)/shard_map/all_gather | solution.py:122
  656.1 6.0 fusion.13
  662.1 0.1 reshape.266
  662.2 11.8 %psum.7 = f32[1,16,8]{2,1,0:T(8,128)S(1)} all-reduce(f32[1,16,8]{2,1,0:T(8,128)S(1)} %reshape.266), channel_id=1, replica_groups=mesh['tensor'=4,'example'=8] {'tensor'}, use_global_device_ids=true, to_apply=%region_7.8 | all-reduce | flops 128 | bytes 1024 | tf_op jit(solution)/shard_map/psum | solution.py:126
  674.0 0.1 fusion.19
  674.1 0.7 copy.31
  (30 shorter events, 0.1 us)
Async XLA Ops:
  6.5 85.9 %copy-start = (bf16[1,512,1024]{2,1,0:T(8,128)(2,1)S(1)}, bf16[1,512,1024]{2,1,0:T(8,128)(2,1)}, u32[]{:S(2)}) copy-start(bf16[1,512,1024]{2,1,0:T(8,128)(2,1)} %param.9) | copy-start | bytes 3145732
  6.5 85.9 %all-gather.8.cloned.1.call-start = ((), (), s32[]{:S(2)}) async-start(), calls=%async_computation.4 | async-start | bytes 5242880 | tf_op jit(solution)/shard_map/all_gather | solution.py:24
  7.3 141.6 %all-gather.10.cloned.1.call-start = ((), (), s32[]{:S(2)}) async-start(), calls=%async_computation.6 | async-start | bytes 9437184 | tf_op jit(solution)/shard_map/all_gather | solution.py:25
  8.0 215.6 %reduce-scatter.3.cloned.1.call-start = ((), (), s32[]{:S(2)}) async-start(), calls=%async_computation.5 | async-start | bytes 9437184 | tf_op jit(solution)/shard_map/reduce_scatter | solution.py:28
  101.5 209.2 %reduce-scatter.5.cloned.1.call-start = ((), (), s32[]{:S(2)}) async-start(), calls=%async_computation.7 | async-start | bytes 5242880 | tf_op jit(solution)/shard_map/reduce_scatter | solution.py:37
  233.8 338.6 %all-gather.14.cloned.1.call-start = ((), (), s32[]{:S(2)}) async-start(), calls=%async_computation.9 | async-start | bytes 5242880 | tf_op jit(solution)/shard_map/all_gather | solution.py:54
  313.5 14.2 %collective-permute-start = (bf16[1024,1,512]{0,2,1:T(8,128)(2,1)S(1)}, bf16[1024,1,512]{0,2,1:T(8,128)(2,1)S(1)}, u32[]{:S(2)}, u32[]{:S(2)}) collective-permute-start(bf16[1024,1,512]{0,2,1:T(8,128)(2,1)S(1)} %get-tuple-element.8), channel_id=1, source_target_pairs={{0,7},{1,0},{2,1},{3,2},{4,3},{5,4},{6,5},{7,6},{8,15},{9,8},{10,9... | collective-permute-start | bytes 3145736 | tf_op jit(solution)/shard_map/ppermute | solution.py:12
  327.6 48.6 %copy-start.2 = (bf16[1024,1,512]{0,2,1:T(8,128)(2,1)}, bf16[1024,1,512]{0,2,1:T(8,128)(2,1)S(1)}, u32[]{:S(2)}) copy-start(bf16[1024,1,512]{0,2,1:T(8,128)(2,1)S(1)} %collective-permute-done) | copy-start | bytes 3145732
  327.9 48.3 %collective-permute-start.1 = (bf16[1024,1,1024]{0,2,1:T(8,128)(2,1)S(1)}, bf16[1024,1,1024]{0,2,1:T(8,128)(2,1)S(1)}, u32[]{:S(2)}, u32[]{:S(2)}) collective-permute-start(bf16[1024,1,1024]{0,2,1:T(8,128)(2,1)S(1)} %pad_maximum_fusion.1), channel_id=1, source_target_pairs={{0,6},{1,7},{2,0},{3,1},{4,2},{5,3},{6,4},{7,5},{8,14},{9,15},{10,... | collective-permute-start | bytes 6291464 | tf_op jit(solution)/shard_map/ppermute | solution.py:12
  378.5 92.6 %collective-permute-start.2 = (bf16[1024,1,2048]{0,2,1:T(8,128)(2,1)}, bf16[1024,1,2048]{0,2,1:T(8,128)(2,1)}, u32[]{:S(2)}, u32[]{:S(2)}) collective-permute-start(bf16[1024,1,2048]{0,2,1:T(8,128)(2,1)} %pad_maximum_fusion), channel_id=1, source_target_pairs={{0,4},{1,5},{2,6},{3,7},{4,0},{5,1},{6,2},{7,3},{8,12},{9,13},{10,... | collective-permute-start | bytes 12582920 | tf_op jit(solution)/shard_map/ppermute | solution.py:12
  379.1 97.8 %copy-start.3 = (bf16[1024,1,512]{0,2,1:T(8,128)(2,1)S(1)}, bf16[1024,1,512]{0,2,1:T(8,128)(2,1)}, u32[]{:S(2)}) copy-start(bf16[1024,1,512]{0,2,1:T(8,128)(2,1)} %copy-done.2) | copy-start | bytes 3145732
  475.7 8.2 %copy-start.9 = (bf16[512,4096]{1,0:T(8,128)(2,1)S(1)}, bf16[512,4096]{1,0:T(8,128)(2,1)}, u32[]{:S(2)}) copy-start(bf16[512,4096]{1,0:T(8,128)(2,1)} %all-gather.8.cloned.1.call-done) | copy-start | bytes 12582916
  483.9 8.4 %copy-start.4 = (bf16[16,8,1024]{2,1,0:T(8,128)(2,1)S(1)}, bf16[16,8,1024]{2,1,0:T(8,128)(2,1)}, u32[]{:S(2)}) copy-start(bf16[16,8,1024]{2,1,0:T(8,128)(2,1)} %param.14) | copy-start | bytes 786436
  484.0 8.5 %copy-start.6 = (s32[8,16]{1,0:T(8,128)S(1)}, s32[8,16]{1,0:T(8,128)}, u32[]{:S(2)}) copy-start(s32[8,16]{1,0:T(8,128)} %param.16) | copy-start | bytes 1540
  484.0 8.5 %copy-start.7 = (s32[128]{0:T(128)S(1)}, s32[128]{0:T(128)}, u32[]{:S(2)}) copy-start(s32[128]{0:T(128)} %param.17) | copy-start | bytes 1540
  484.0 8.5 %copy-start.8 = (s32[128]{0:T(128)S(1)}, s32[128]{0:T(128)}, u32[]{:S(2)}) copy-start(s32[128]{0:T(128)} %param.15) | copy-start | bytes 1540
  495.0 13.2 %all-to-all-start.1 = ((bf16[8,4,8192]{2,1,0:T(4,128)(2,1)}), bf16[8,4,8192]{2,1,0:T(4,128)(2,1)S(1)}, u32[]{:S(2)}, u32[]{:S(2)}) async-start(bf16[8,4,8192]{2,1,0:T(4,128)(2,1)} %copy.28), calls=%async_computation.3 | async-start | bytes 1048576 | tf_op jit(solution)/shard_map/all_to_all | solution.py:113
  498.5 101.8 %all-gather.12.cloned.1.call-start = ((), (), s32[]{:S(2)}) async-start(), calls=%async_computation.8 | async-start | bytes 1310720 | tf_op jit(solution)/shard_map/all_gather | solution.py:117
  509.4 73.2 %copy-start.5 = (bf16[16,8,1024]{2,1,0:T(8,128)(2,1)S(1)}, bf16[16,8,1024]{2,1,0:T(8,128)(2,1)}, u32[]{:S(2)}) copy-start(bf16[16,8,1024]{2,1,0:T(8,128)(2,1)} %param.13) | copy-start | bytes 786436
  509.4 146.7 %all-gather.16.cloned.1.call-start = ((), (), s32[]{:S(2)}) async-start(), calls=%async_computation.10 | async-start | bytes 9437184 | tf_op jit(solution)/shard_map/all_gather | solution.py:122
  582.6 92.2 %copy-start.1 = (bf16[1,512,1024]{2,1,0:T(8,128)(2,1)S(1)}, bf16[1,512,1024]{2,1,0:T(8,128)(2,1)}, u32[]{:S(2)}) copy-start(bf16[1,512,1024]{2,1,0:T(8,128)(2,1)} %param.9) | copy-start | bytes 3145732
  584.2 13.4 %all-to-all-start = ((bf16[8,4,8192]{2,1,0:T(4,128)(2,1)}), bf16[8,4,8192]{2,1,0:T(4,128)(2,1)S(1)}, u32[]{:S(2)}, u32[]{:S(2)}) async-start(bf16[8,4,8192]{2,1,0:T(4,128)(2,1)} %copy.24), calls=%async_computation | async-start | bytes 1048576 | tf_op jit(solution)/shard_map/all_to_all | solution.py:112
Sparse Core Ops, SparseCore 0:
  8.9 83.4 all-gather.7
  94.3 54.4 all-gather.9
  152.3 71.2 reduce-scatter.2
  233.9 76.7 reduce-scatter.4
  492.4 79.9 all-gather.13
  573.8 26.4 all-gather.11
  602.2 53.8 all-gather.15
